TPU v7x, 32 devices: a whole 2x2x4 slice. The times are simulated.
32 devices in a mesh: kv: 4 (over y, x), seq: 8 (over z, core).
Axes of the slice: x: 2, y: 2, z: 4, core: 2. Of those that a mesh axis runs over, the one named last changes fastest.
Arguments:
- queries: bfloat16 [1024, 12288], P('seq', 'kv'), may hold values from -400 to 400
- cache_keys: bfloat16 [8192, 768], P('seq', 'kv'), may hold values from -6 to 6
- cache_values: bfloat16 [8192, 512], P('seq', 'kv'), may hold values from -6 to 6
- incoming_keys: bfloat16 [1024, 768], P('seq', 'kv'), may hold values from -6 to 6
- new_values: bfloat16 [1024, 512], P('seq', 'kv'), may hold values from -6 to 6
- comp_key_weight: bfloat16 [6144, 192], P('kv'), may hold values from -0.078125 to 0.078125
- comp_value_weight: bfloat16 [4096, 128], P('kv'), may hold values from -0.09375 to 0.09375
- select_blocks: int32 [32, 4, 16], P('seq', 'kv'), may hold values from 0 to 127, as said below
- gate_weight: bfloat16 [64, 192, 3], P('kv'), may hold values from -0.4375 to 0.4375
Outputs:
- attended: bfloat16 [1024, 8192], P('seq', 'kv')
Inputs may be any that keep to these rules, and one draw needn't show every extreme that they name: `select_blocks`: each row names 16 different blocks. For each KV group, the rows of one device of seq (4 tiles) name blocks of any one cache shard (the 16 blocks of one index of seq) at most 16 times in all, and in every draw the rows of every device name one shard's blocks exactly 16 times.
All inputs are finite; a program needn't handle non-finite values.
Results may differ from a plain program's by a relative error of at most 0.012.
Values may be sent and summed in bfloat16 or wider, within the bound.
A program may use at most 128 MiB of HBM per device.

v0:
```python
import jax
import jax.numpy as jnp
from jax import lax
from jax.sharding import PartitionSpec as P

CMP_STRIDE = 16
SEL_BLOCK = 64
WINDOW = 512
MASKED = -1e30


def passed_along(block, axis, distance):
    devices = range(lax.axis_size(axis))
    route = [((i - distance) % len(devices), i) for i in devices]
    return lax.ppermute(block, axis, route)


def from_behind(x, axis, by):
    peers = lax.axis_size(axis)
    pairs = [(i, i + by) for i in range(peers) if 0 <= i + by < peers]
    return lax.ppermute(x, axis, pairs)


def pack_rows(keys, values):
    return jnp.concatenate([keys.reshape(-1), values.reshape(-1)])


def unpack_rows(flat, count, key_width, value_width):
    keys = flat[: count * key_width].reshape(count, key_width)
    values = flat[count * key_width : count * (key_width + value_width)].reshape(count, value_width)
    return (keys, values)


def finish_rows(scores, values):
    top = jnp.max(scores, axis=-1, keepdims=True)
    weights = jnp.exp(scores - top)
    total = jnp.sum(weights, axis=-1, keepdims=True)
    mixed = jnp.matmul(weights.astype(jnp.bfloat16), values, preferred_element_type=jnp.float32)
    return mixed / total


def shards(
    queries,
    cache_keys,
    cache_values,
    incoming_keys,
    new_values,
    comp_key_weight,
    comp_value_weight,
    select_blocks,
    gate_weight,
):
    heads, key_width, _ = gate_weight.shape
    value_width = cache_values.shape[1]
    query_count = queries.shape[0]
    cache_count = cache_keys.shape[0]
    ranks = lax.axis_size("seq")
    place = lax.axis_index("seq")
    scale = key_width ** (-0.5)
    rows = queries.reshape(query_count * heads, key_width)
    row_total = rows.shape[0]
    stretch_pos = place * query_count + jnp.arange(query_count, dtype=jnp.int32)
    lookback_length = -(-WINDOW // query_count)
    weight_keys, weight_values = (
        lax.all_gather(comp_key_weight, "kv", axis=0, tiled=True),
        lax.all_gather(comp_value_weight, "kv", axis=0, tiled=True),
    )
    tail_pack = pack_rows(cache_keys[cache_count - WINDOW :], cache_values[cache_count - WINDOW :])
    moved_tail = passed_along(tail_pack, "seq", 1)
    before_keys, before_values = unpack_rows(moved_tail, WINDOW, key_width, value_width)
    edge_keys = before_keys[WINDOW - CMP_STRIDE :]
    edge_values = before_values[WINDOW - CMP_STRIDE :]
    held_tail = jnp.where(place == 0, moved_tail, jnp.zeros_like(moved_tail))
    tail_size = held_tail.shape[0]
    tail_flat = held_tail
    near_keys = []
    near_values = []
    nearby_positions = []
    near_valid = []
    own = pack_rows(incoming_keys, new_values)
    own_size = own.shape[0]
    for back in range(lookback_length, 0, -1):
        moved = from_behind(jnp.concatenate([own, held_tail]), "seq", back)
        got_keys, got_values = unpack_rows(moved, query_count, key_width, value_width)
        tail_flat = jnp.where(place == back, moved[own_size : own_size + tail_size], tail_flat)
        near_keys.append(got_keys)
        near_values.append(got_values)
        nearby_positions.append(
            (place - back) * query_count + jnp.arange(query_count, dtype=jnp.int32)
        )
        near_valid.append(jnp.broadcast_to(place >= back, (query_count,)))
    tail_keys, tail_values = unpack_rows(tail_flat, WINDOW, key_width, value_width)
    near_keys.append(tail_keys)
    near_values.append(tail_values)
    nearby_positions.append(jnp.arange(WINDOW, dtype=jnp.int32) - WINDOW)
    near_valid.append(jnp.ones((WINDOW,), dtype=bool))
    near_keys.append(incoming_keys)
    near_values.append(new_values)
    nearby_positions.append(stretch_pos)
    near_valid.append(jnp.ones((query_count,), dtype=bool))
    half_keys = CMP_STRIDE * key_width
    half_values = CMP_STRIDE * value_width
    lead_keys = jnp.concatenate([edge_keys, cache_keys[: cache_count - CMP_STRIDE]]).reshape(
        -1, half_keys
    )
    lead_values = jnp.concatenate([edge_values, cache_values[: cache_count - CMP_STRIDE]]).reshape(
        -1, half_values
    )
    comp_keys = (
        jnp.dot(lead_keys, weight_keys[:half_keys], preferred_element_type=jnp.float32)
        + jnp.dot(
            cache_keys.reshape(-1, half_keys),
            weight_keys[half_keys:],
            preferred_element_type=jnp.float32,
        )
    ).astype(jnp.bfloat16)
    comp_values = (
        jnp.dot(lead_values, weight_values[:half_values], preferred_element_type=jnp.float32)
        + jnp.dot(
            cache_values.reshape(-1, half_values),
            weight_values[half_values:],
            preferred_element_type=jnp.float32,
        )
    ).astype(jnp.bfloat16)
    start = jnp.int32(0)
    top = jnp.full((row_total,), MASKED, jnp.float32)
    total = jnp.zeros((row_total,), jnp.float32)
    summed = jnp.zeros((row_total, value_width), jnp.float32)
    keys = lax.all_gather(comp_keys, "seq", axis=0, tiled=True)
    values = lax.all_gather(comp_values, "seq", axis=0, tiled=True)
    length = keys.shape[0]
    block = length
    for size in (1024, 512, 256, 128):
        if length % size == 0:
            block = size
            break
    for index in range(length // block):
        key_block = keys[index * block : (index + 1) * block]
        value_block = values[index * block : (index + 1) * block]
        scores = (
            jnp.einsum("rd,kd->rk", rows, key_block, preferred_element_type=jnp.float32) * scale
        )
        key_at = start + index * block + jnp.arange(block, dtype=jnp.int32)
        scores = jnp.where(key_at[None, :] > 0, scores, MASKED)
        newtop = jnp.maximum(top, jnp.max(scores, axis=1))
        factor = jnp.exp(top - newtop)
        weights = jnp.exp(scores - newtop[:, None])
        total = total * factor + jnp.sum(weights, axis=1)
        summed = summed * factor[:, None] + jnp.dot(
            weights.astype(jnp.bfloat16), value_block, preferred_element_type=jnp.float32
        )
        top = newtop
    top, total, summed = (top, total, summed)
    compressed_out = summed / total[:, None]
    chosen = select_blocks.reshape(-1)
    shard_blocks = cache_count // SEL_BLOCK
    capacity = max(2, 2 * chosen.shape[0] // ranks)
    owner = chosen // shard_blocks
    local = chosen - owner * shard_blocks
    onehot = (owner[:, None] == jnp.arange(ranks, dtype=jnp.int32)[None, :]).astype(jnp.int32)
    position = jnp.sum((jnp.cumsum(onehot, axis=0) - 1) * onehot, axis=1)
    request = jnp.full((ranks, capacity), -1, jnp.int32).at[owner, position].set(local)
    key_blocks = cache_keys.reshape(shard_blocks, SEL_BLOCK, key_width)
    value_block_list = cache_values.reshape(shard_blocks, SEL_BLOCK, value_width)
    safe = jnp.clip(
        lax.all_to_all(request, "seq", split_axis=0, concat_axis=0, tiled=True), 0, shard_blocks - 1
    )
    got_keys = lax.all_to_all(key_blocks[safe], "seq", split_axis=0, concat_axis=0, tiled=True)
    got_values = lax.all_to_all(
        value_block_list[safe], "seq", split_axis=0, concat_axis=0, tiled=True
    )
    where_at = owner * capacity + position
    tile_count = select_blocks.shape[0]
    gathered_keys = got_keys.reshape(ranks * capacity, SEL_BLOCK, key_width)[where_at]
    picked_values = got_values.reshape(ranks * capacity, SEL_BLOCK, value_width)[where_at]
    gathered_keys, picked_values = (
        gathered_keys.reshape(tile_count, -1, key_width),
        picked_values.reshape(tile_count, -1, value_width),
    )
    tile_count = gathered_keys.shape[0]
    tile_row_count = rows.reshape(tile_count, -1, key_width)
    tile_scores = (
        jnp.einsum(
            "izu,ixu->izx", tile_row_count, gathered_keys, preferred_element_type=jnp.float32
        )
        * scale
    )
    selected_out = finish_rows(tile_scores, picked_values).reshape(row_total, value_width)
    context_keys = jnp.concatenate(near_keys)
    context_values = jnp.concatenate(near_values)
    context_positions = jnp.concatenate(nearby_positions)
    context_valid = jnp.concatenate(near_valid)
    sliding_scores = (
        jnp.einsum("rd,kd->rk", rows, context_keys, preferred_element_type=jnp.float32) * scale
    )
    allowed = (
        context_valid[None, :]
        & (context_positions[None, :] <= stretch_pos[:, None])
        & (context_positions[None, :] > stretch_pos[:, None] - WINDOW)
    )
    sliding_scores = jnp.where(
        allowed[:, None, :], sliding_scores.reshape(query_count, heads, -1), MASKED
    )
    window_out = finish_rows(sliding_scores.reshape(row_total, -1), context_values)
    logits = jnp.einsum(
        "thd,hdb->thb",
        queries.reshape(query_count, heads, key_width),
        gate_weight,
        preferred_element_type=jnp.float32,
    )
    gates = jax.nn.sigmoid(logits)
    mixed = (
        gates[:, :, 0:1] * compressed_out.reshape(query_count, heads, value_width)
        + gates[:, :, 1:2] * selected_out.reshape(query_count, heads, value_width)
        + gates[:, :, 2:3] * window_out.reshape(query_count, heads, value_width)
    )
    return mixed.astype(jnp.bfloat16).reshape(query_count, heads * value_width)


def solution(mesh):
    placed = (
        P("seq", "kv"),
        P("seq", "kv"),
        P("seq", "kv"),
        P("seq", "kv"),
        P("seq", "kv"),
        P("kv", None),
        P("kv", None),
        P("seq", "kv", None),
        P("kv", None, None),
    )
    return jax.shard_map(
        shards, mesh=mesh, in_specs=placed, out_specs=P("seq", "kv"), check_vma=False
    )
```

profile of v0, /device:TPU:0, one launch (start us, length us, event | category | flops | bytes accessed | tf_op | source)
XLA Modules:
  0.0 310.4 jit_solution(10423262976556319975)
XLA Ops:
  14.6 10.2 %scatter_fusion = s32[8,16]{1,0:T(8,128)} fusion(s32[8,16]{1,0:T(8,128)} %broadcast_in_dim.83, s32[64]{0:T(128)S(1)} %fusion.59, s32[64]{0:T(128)S(1)} %get-tuple-element.7), kind=kCustom, calls=%fused_computation.4 | custom fusion | bytes 1280 | tf_op jit(solution)/shard_map/scatter | solution.py:162
  24.7 6.3 %all-to-all-start = ((s32[8,1,16]{2,1,0:T(1,128)}), s32[8,1,16]{2,1,0:T(1,128)}, u32[]{:S(2)}, u32[]{:S(2)}) async-start(s32[8,1,16]{2,1,0:T(1,128)} %bitcast.10), calls=%async_computation | async-start | bytes 8192 | tf_op jit(solution)/shard_map/all_to_all | solution.py:166
  32.0 2.1 reshape.394
  34.2 2.1 reshape_reshape.6
  43.5 2.5 copy.51
  47.3 1.4 copy.36
  50.9 2.8 gather_fusion
  53.7 2.2 gather_fusion.2
  55.9 5.1 %all-to-all-start.2 = ((bf16[8,16,64,128]{3,2,1,0:T(8,128)(2,1)}), bf16[8,16,64,128]{3,2,1,0:T(8,128)(2,1)}, u32[]{:S(2)}, u32[]{:S(2)}) async-start(bf16[8,16,64,128]{3,2,1,0:T(8,128)(2,1)} %bitcast.113), calls=%async_computation.2 | async-start | bytes 4194304 | tf_op jit(solution)/shard_map/all_to_all | solution.py:169
  62.8 4.6 %collective-permute-start.1 = (bf16[204800]{0:T(1024)(128)(2,1)}, bf16[204800]{0:T(1024)(128)(2,1)}, u32[]{:S(2)}, u32[]{:S(2)}) collective-permute-start(bf16[204800]{0:T(1024)(128)(2,1)} %pad_maximum_fusion), channel_id=1, source_target_pairs={{0,4},{1,5},{2,6},{3,7},{8,12},{9,13},{10,14},{11,15},{16,20},{17,... | collective-permute-start | bytes 1228808 | tf_op jit(solution)/shard_map/ppermute | solution.py:21
  67.4 3.6 %collective-permute-start.2 = (bf16[204800]{0:T(1024)(128)(2,1)}, bf16[204800]{0:T(1024)(128)(2,1)}, u32[]{:S(2)}, u32[]{:S(2)}) collective-permute-start(bf16[204800]{0:T(1024)(128)(2,1)} %pad_maximum_fusion), channel_id=1, source_target_pairs={{0,3},{1,4},{2,5},{3,6},{4,7},{8,11},{9,12},{10,13},{11,14},{12,15... | collective-permute-start | bytes 1228808 | tf_op jit(solution)/shard_map/ppermute | solution.py:21
  71.0 2.6 collective-permute-start.3
  73.6 2.1 collective-permute-start.4
  81.9 23.0 %collective-permute-done.1 = bf16[204800]{0:T(1024)(128)(2,1)} collective-permute-done((bf16[204800]{0:T(1024)(128)(2,1)}, bf16[204800]{0:T(1024)(128)(2,1)}, u32[]{:S(2)}, u32[]{:S(2)}) %collective-permute-start.1) | collective-permute-done | bytes 409632 | tf_op jit(solution)/shard_map/ppermute | solution.py:21
  106.3 7.4 %collective-permute-done.2 = bf16[204800]{0:T(1024)(128)(2,1)} collective-permute-done((bf16[204800]{0:T(1024)(128)(2,1)}, bf16[204800]{0:T(1024)(128)(2,1)}, u32[]{:S(2)}, u32[]{:S(2)}) %collective-permute-start.2) | collective-permute-done | bytes 409632 | tf_op jit(solution)/shard_map/ppermute | solution.py:21
  115.0 7.4 %collective-permute-done.3 = bf16[204800]{0:T(1024)(128)(2,1)} collective-permute-done((bf16[204800]{0:T(1024)(128)(2,1)}, bf16[204800]{0:T(1024)(128)(2,1)}, u32[]{:S(2)}, u32[]{:S(2)}) %collective-permute-start.3) | collective-permute-done | bytes 409632 | tf_op jit(solution)/shard_map/ppermute | solution.py:21
  122.5 1.4 fusion.49
  130.5 33.3 %all-to-all-start.1 = ((bf16[8,16,64,192]{3,2,1,0:T(8,128)(2,1)}), bf16[8,16,64,192]{3,2,1,0:T(8,128)(2,1)}, u32[]{:S(2)}, u32[]{:S(2)}) async-start(bf16[8,16,64,192]{3,2,1,0:T(8,128)(2,1)} %bitcast.110), calls=%async_computation.1 | async-start | bytes 8388608 | tf_op jit(solution)/shard_map/all_to_all | solution.py:168
  164.4 1.4 constant_dynamic-update-slice_fusion.7
  165.8 3.2 %fusion.65 = (f32[2048]{0:T(1024)S(1)}, f32[2048,1152]{0,1:T(8,128)S(1)}) fusion(pred[2048,1152]{0,1:T(32,128)(4,1)S(1)} %copy.51, bf16[1152,192]{1,0:T(8,128)(2,1)S(1)} %constant_dynamic-update-slice_fusion.1, bf16[2048,192]{1,0:T(8,128)(2,1)} %reshape.394), kind=kOutput, calls=%fused_computation.126 | convolution fusion | flops 913045504 | bytes 13033472 | tf_op jit(solution)/shard_map/rd,kd->rk/dot_general | solution.py:194
  170.4 1.8 fusion.16
  176.0 88.1 %all_gather.15 = bf16[512,128]{1,0:T(8,128)(2,1)S(1)} all-gather(bf16[64,128]{1,0:T(8,128)(2,1)S(1)} %fusion.37), channel_id=1, replica_groups=mesh['kv'=4,'seq'=8] {'seq'}, dimensions={0}, use_global_device_ids=true | all-gather | bytes 147456 | tf_op jit(solution)/shard_map/all_gather | solution.py:130
  264.1 1.8 fusion.23
  265.9 1.9 fusion.30
  267.8 14.4 %all_gather.13 = bf16[512,192]{1,0:T(8,128)(2,1)S(1)} all-gather(bf16[64,192]{1,0:T(8,128)(2,1)S(1)} %fusion.30), channel_id=1, replica_groups=mesh['kv'=4,'seq'=8] {'seq'}, dimensions={0}, use_global_device_ids=true | all-gather | bytes 221184 | tf_op jit(solution)/shard_map/all_gather | solution.py:129
  284.0 1.5 fusion.15
  286.7 3.4 %gather_fusion.3 = bf16[64,64,128]{2,1,0:T(8,128)(2,1)} fusion(bf16[128,64,128]{2,1,0:T(8,128)(2,1)} %bitcast.20, s32[1024]{0:T(1024)} %pad_clamp_fusion), kind=kCustom, calls=%fused_computation.3 | custom fusion | bytes 2097408 | tf_op jit(solution)/shard_map/gather | solution.py:175
  290.1 3.0 gather_fusion.1
  294.4 1.4 fusion.3
  295.8 3.2 %fusion.41 = f32[4,512,128]{2,1,0:T(8,128)} fusion(bf16[4,1024,128]{2,1,0:T(8,128)(2,1)S(1)} %bitcast.119, f32[4,1024,512]{2,1,0:T(8,128)S(1)} %get-tuple-element.17, f32[4,512]{1,0:T(4,128)S(1)} %get-tuple-element.16, f32[4,512]{1,0:T(4,128)S(1)} %fusion.3), kind=kOutput, calls=%fused_computation.50 | convolution fusion | flops 543424512 | bytes 10502144 | tf_op jit(solution)/shard_map/dot_general | solution.py:38
  299.0 1.5 reshape_reshape.7
  301.6 1.9 fusion.39
  (153 shorter events, 47.7 us)
Async XLA Ops:
  6.5 25.3 %copy-start.6 = (bf16[1024,192]{0,1:T(8,128)(2,1)S(1)}, bf16[1024,192]{0,1:T(8,128)(2,1)}, u32[]{:S(2)}) copy-start(bf16[1024,192]{0,1:T(8,128)(2,1)} %param.10) | copy-start | bytes 1179652
  6.5 25.5 %copy-start.1 = (bf16[128,3072]{1,0:T(8,128)(2,1)S(1)}, bf16[128,3072]{1,0:T(8,128)(2,1)}, u32[]{:S(2)}) copy-start(bf16[128,3072]{1,0:T(8,128)(2,1)} %param.9) | copy-start | bytes 2359300
  6.5 166.9 %all-gather.5.cloned.1.call-start = ((), (), s32[]{:S(2)}) async-start(), calls=%async_computation.4 | async-start | bytes 1310720 | tf_op jit(solution)/shard_map/all_gather | solution.py:66
  10.3 28.9 %copy-start.18 = (bf16[16,192,3]{1,0,2:T(8,128)(2,1)S(1)}, bf16[16,192,3]{1,0,2:T(8,128)(2,1)}, u32[]{:S(2)}) copy-start(bf16[16,192,3]{1,0,2:T(8,128)(2,1)} %param.17) | copy-start | bytes 55300
  10.3 50.6 %collective-permute-start = (bf16[163840]{0:T(1024)(128)(2,1)}, bf16[163840]{0:T(1024)(128)(2,1)}, u32[]{:S(2)}, u32[]{:S(2)}) collective-permute-start(bf16[163840]{0:T(1024)(128)(2,1)} %pad_maximum_fusion.2), channel_id=1, source_target_pairs={{7,0},{0,1},{1,2},{2,3},{3,4},{4,5},{5,6},{6,7},{15,8},{8,9},{9,10... | collective-permute-start | bytes 983048 | tf_op jit(solution)/shard_map/ppermute | solution.py:15
  24.7 15.7 %copy-start = (bf16[1024,128]{1,0:T(8,128)(2,1)S(1)}, bf16[1024,128]{1,0:T(8,128)(2,1)}, u32[]{:S(2)}) copy-start(bf16[1024,128]{1,0:T(8,128)(2,1)} %param.11) | copy-start | bytes 786436
  24.7 25.5 %all-to-all-start = ((s32[8,1,16]{2,1,0:T(1,128)}), s32[8,1,16]{2,1,0:T(1,128)}, u32[]{:S(2)}, u32[]{:S(2)}) async-start(s32[8,1,16]{2,1,0:T(1,128)} %bitcast.10), calls=%async_computation | async-start | bytes 8192 | tf_op jit(solution)/shard_map/all_to_all | solution.py:166
  31.0 233.1 %all-gather.3.cloned.1.call-start = ((), (), s32[]{:S(2)}) async-start(), calls=%async_computation.3 | async-start | bytes 2949120 | tf_op jit(solution)/shard_map/all_gather | solution.py:65
  31.7 10.3 %copy-start.17 = (bf16[128,192]{0,1:T(8,128)(2,1)S(1)}, bf16[128,192]{0,1:T(8,128)(2,1)}, u32[]{:S(2)}) copy-start(bf16[128,192]{0,1:T(8,128)(2,1)} %param.12) | copy-start | bytes 147460
  42.1 1.4 copy-start.9
  53.7 8.3 %copy-start.15 = (bf16[24576]{0:T(1024)(128)(2,1)S(1)}, bf16[24576]{0:T(1024)(128)(2,1)}, u32[]{:S(2)}) copy-start(bf16[24576]{0:T(1024)(128)(2,1)} %reshape.406) | copy-start | bytes 147460
  53.7 8.3 %copy-start.16 = (bf16[128,128]{1,0:T(8,128)(2,1)S(1)}, bf16[128,128]{1,0:T(8,128)(2,1)}, u32[]{:S(2)}) copy-start(bf16[128,128]{1,0:T(8,128)(2,1)} %param.13) | copy-start | bytes 98308
  55.9 74.6 %all-to-all-start.2 = ((bf16[8,16,64,128]{3,2,1,0:T(8,128)(2,1)}), bf16[8,16,64,128]{3,2,1,0:T(8,128)(2,1)}, u32[]{:S(2)}, u32[]{:S(2)}) async-start(bf16[8,16,64,128]{3,2,1,0:T(8,128)(2,1)} %bitcast.113), calls=%async_computation.2 | async-start | bytes 4194304 | tf_op jit(solution)/shard_map/all_to_all | solution.py:169
  62.8 42.1 %collective-permute-start.1 = (bf16[204800]{0:T(1024)(128)(2,1)}, bf16[204800]{0:T(1024)(128)(2,1)}, u32[]{:S(2)}, u32[]{:S(2)}) collective-permute-start(bf16[204800]{0:T(1024)(128)(2,1)} %pad_maximum_fusion), channel_id=1, source_target_pairs={{0,4},{1,5},{2,6},{3,7},{8,12},{9,13},{10,14},{11,15},{16,20},{17,... | collective-permute-start | bytes 1228808 | tf_op jit(solution)/shard_map/ppermute | solution.py:21
  67.4 46.3 %collective-permute-start.2 = (bf16[204800]{0:T(1024)(128)(2,1)}, bf16[204800]{0:T(1024)(128)(2,1)}, u32[]{:S(2)}, u32[]{:S(2)}) collective-permute-start(bf16[204800]{0:T(1024)(128)(2,1)} %pad_maximum_fusion), channel_id=1, source_target_pairs={{0,3},{1,4},{2,5},{3,6},{4,7},{8,11},{9,12},{10,13},{11,14},{12,15... | collective-permute-start | bytes 1228808 | tf_op jit(solution)/shard_map/ppermute | solution.py:21
  71.0 51.5 %collective-permute-start.3 = (bf16[204800]{0:T(1024)(128)(2,1)}, bf16[204800]{0:T(1024)(128)(2,1)}, u32[]{:S(2)}, u32[]{:S(2)}) collective-permute-start(bf16[204800]{0:T(1024)(128)(2,1)} %pad_maximum_fusion), channel_id=1, source_target_pairs={{0,2},{1,3},{2,4},{3,5},{4,6},{5,7},{8,10},{9,11},{10,12},{11,13},... | collective-permute-start | bytes 1228808 | tf_op jit(solution)/shard_map/ppermute | solution.py:21
  73.6 48.9 %collective-permute-start.4 = (bf16[204800]{0:T(1024)(128)(2,1)}, bf16[204800]{0:T(1024)(128)(2,1)}, u32[]{:S(2)}, u32[]{:S(2)}) collective-permute-start(bf16[204800]{0:T(1024)(128)(2,1)} %pad_maximum_fusion), channel_id=1, source_target_pairs={{0,1},{1,2},{2,3},{3,4},{4,5},{5,6},{6,7},{8,9},{9,10},{10,11},{11... | collective-permute-start | bytes 1228808 | tf_op jit(solution)/shard_map/ppermute | solution.py:21
  130.5 35.4 %copy-start.10 = (bf16[128,192]{1,0:T(8,128)(2,1)S(1)}, bf16[128,192]{1,0:T(8,128)(2,1)}, u32[]{:S(2)}) copy-start(bf16[128,192]{1,0:T(8,128)(2,1)} %copy-done.9) | copy-start | bytes 147460
  130.5 159.6 %all-to-all-start.1 = ((bf16[8,16,64,192]{3,2,1,0:T(8,128)(2,1)}), bf16[8,16,64,192]{3,2,1,0:T(8,128)(2,1)}, u32[]{:S(2)}, u32[]{:S(2)}) async-start(bf16[8,16,64,192]{3,2,1,0:T(8,128)(2,1)} %bitcast.110), calls=%async_computation.1 | async-start | bytes 8388608 | tf_op jit(solution)/shard_map/all_to_all | solution.py:168
  169.0 1.4 copy-start.19
  170.4 4.3 %copy-start.8 = (bf16[64,2048]{1,0:T(8,128)(2,1)S(1)}, bf16[64,2048]{1,0:T(8,128)(2,1)}, u32[]{:S(2)}) copy-start(bf16[64,2048]{1,0:T(8,128)(2,1)} %reshape.396) | copy-start | bytes 786436
  170.4 93.7 %copy-start.11 = (bf16[64,3072]{1,0:T(8,128)(2,1)S(1)}, bf16[64,3072]{1,0:T(8,128)(2,1)}, u32[]{:S(2)}) copy-start(bf16[64,3072]{1,0:T(8,128)(2,1)} %reshape.393) | copy-start | bytes 1179652
  172.2 109.9 %copy-start.3 = (bf16[2048,192]{1,0:T(8,128)(2,1)S(1)}, bf16[2048,192]{1,0:T(8,128)(2,1)}, u32[]{:S(2)}) copy-start(bf16[2048,192]{1,0:T(8,128)(2,1)} %reshape.394) | copy-start | bytes 2359300
  172.3 109.9 %copy-start.20 = (pred[512]{0:T(512)(128)(4,1)S(1)}, pred[512]{0:T(512)(128)(4,1)}, u32[]{:S(2)}) copy-start(pred[512]{0:T(512)(128)(4,1)} %iota_compare_fusion.1) | copy-start | bytes 1540
  285.5 7.6 %copy-start.2 = (bf16[4,512,192]{2,1,0:T(8,128)(2,1)S(1)}, bf16[4,512,192]{2,1,0:T(8,128)(2,1)}, u32[]{:S(2)}) copy-start(bf16[4,512,192]{2,1,0:T(8,128)(2,1)} %reshape_reshape.6) | copy-start | bytes 2359300
  294.4 1.4 copy-start.7
  295.8 4.7 %copy-start.12 = (f32[128,16]{1,0:T(8,128)S(1)}, f32[128,16]{1,0:T(8,128)}, u32[]{:S(2)}) copy-start(f32[128,16]{1,0:T(8,128)} %copy.36) | copy-start | bytes 24580
  295.8 5.1 %copy-start.13 = (f32[128,16]{1,0:T(8,128)S(1)}, f32[128,16]{1,0:T(8,128)}, u32[]{:S(2)}) copy-start(f32[128,16]{1,0:T(8,128)} %copy.41) | copy-start | bytes 24580
  299.0 2.2 copy-start.14
  299.0 2.6 copy-start.4
  299.0 2.6 copy-start.5
Sparse Core Ops, SparseCore 0:
  9.2 29.2 all-gather.4
  40.3 37.2 all-gather.2
where the time goes:
time: 312 us; the launch traced here: 310 us
  blocking collectives  103 us (33%)
  local copies, waits for them, and re-layouts  62.8 us (20%)
  starting transfers between devices  58.1 us (19%)
  waiting for transfers between devices  39.3 us (13%)
  matrix products  18.3 us (6%)
  other arithmetic  15.4 us (5%)
  between operations  14 us (4%)
    all_gather x1, blocking collectives, shards(): values = lax.all_gather(comp_values, 'seq', axis=0, tiled=True)  88.1 us
    ppermute x4, waiting for transfers between devices, from_behind(): return lax.ppermute(x, axis, pairs)  37.8 us
    all_to_all x1, starting transfers between devices, shards(): lax.all_to_all(key_blocks[safe], 'seq', split_axis=0, concat_axis=0, tile...  33.3 us
    all_gather x1, blocking collectives, shards(): keys = lax.all_gather(comp_keys, 'seq', axis=0, tiled=True)  14.4 us
    ppermute x4, starting transfers between devices, from_behind(): return lax.ppermute(x, axis, pairs)  12.9 us
    scatter x1, local copies, waits for them, and re-layouts, shards(): jnp.full((ranks, capacity), -1, jnp.int32).at[owner, position].set(local)  10.2 us
    unnamed x61, local copies, waits for them, and re-layouts  8.66 us
    all_to_all x1, starting transfers between devices, shards(): lax.all_to_all(request, 'seq', split_axis=0, concat_axis=0, tiled=True)  6.28 us
  transfers between devices with their start and end apart: 10, of which 3 were waited for; matrix products, arithmetic and copies ran while one was open for 27% of the time, Pallas kernels for 0%

commit v1 on v0

--- a/solution.py
+++ b/solution.py
@@ -126,8 +126,13 @@
     top = jnp.full((row_total,), MASKED, jnp.float32)
     total = jnp.zeros((row_total,), jnp.float32)
     summed = jnp.zeros((row_total, value_width), jnp.float32)
-    keys = lax.all_gather(comp_keys, "seq", axis=0, tiled=True)
-    values = lax.all_gather(comp_values, "seq", axis=0, tiled=True)
+    keys, values = jnp.split(
+        lax.all_gather(
+            jnp.concatenate([comp_keys, comp_values], axis=1), "seq", axis=0, tiled=True
+        ),
+        [comp_keys.shape[1]],
+        axis=1,
+    )
     length = keys.shape[0]
     block = length
     for size in (1024, 512, 256, 128):

time: 312 us -> 291 us (0.933)
  blocking collectives: 103 us -> 81.4 us
    all_gather x2 -> x1, blocking collectives: 103 us -> 81.4 us  [shards(): lax.all_gather(jnp.concatenate([comp_keys, comp_values], axis=1), 'seq',...]
  transfers between devices with their start and end apart: 10 -> 10, of which waited for: 3 -> 3; matrix products, arithmetic and copies ran while one was open for 27% -> 29% of each run, Pallas kernels for 0% -> 0%
where the time goes in v1:
time: 291 us; the launch traced here: 289 us
  blocking collectives  81.4 us (28%)
  local copies, waits for them, and re-layouts  61.9 us (21%)
  starting transfers between devices  57.9 us (20%)
  waiting for transfers between devices  39.4 us (14%)
  matrix products  19.4 us (7%)
  other arithmetic  15.5 us (5%)
  between operations  14 us (5%)
    all_gather x1, blocking collectives, shards(): lax.all_gather(jnp.concatenate([comp_keys, comp_values], axis=1), 'seq',...  81.4 us
    ppermute x4, waiting for transfers between devices, from_behind(): return lax.ppermute(x, axis, pairs)  37.9 us
    all_to_all x1, starting transfers between devices, shards(): lax.all_to_all(key_blocks[safe], 'seq', split_axis=0, concat_axis=0, tile...  33.3 us
    ppermute x4, starting transfers between devices, from_behind(): return lax.ppermute(x, axis, pairs)  12.9 us
    scatter x1, local copies, waits for them, and re-layouts, shards(): jnp.full((ranks, capacity), -1, jnp.int32).at[owner, position].set(local)  10.2 us
    unnamed x61, local copies, waits for them, and re-layouts  8.63 us
    all_to_all x1, starting transfers between devices, shards(): lax.all_to_all(request, 'seq', split_axis=0, concat_axis=0, tiled=True)  6.14 us
    dot_general x2, matrix products, finish_rows(): jnp.matmul(weights.astype(jnp.bfloat16), values, preferred_element_type=j...  6 us
  transfers between devices with their start and end apart: 10, of which 3 were waited for; matrix products, arithmetic and copies ran while one was open for 29% of the time, Pallas kernels for 0%

profile of v1, /device:TPU:0, one launch (start us, length us, event | category | flops | bytes accessed | tf_op | source)
XLA Modules:
  0.0 289.5 jit_solution(2934884611113679746)
XLA Ops:
  14.5 10.2 %scatter_fusion = s32[8,16]{1,0:T(8,128)} fusion(s32[8,16]{1,0:T(8,128)} %broadcast_in_dim.83, s32[64]{0:T(128)S(1)} %fusion.62, s32[64]{0:T(128)S(1)} %get-tuple-element.7), kind=kCustom, calls=%fused_computation.4 | custom fusion | bytes 1280 | tf_op jit(solution)/shard_map/scatter | solution.py:167
  24.7 6.1 %all-to-all-start = ((s32[8,1,16]{2,1,0:T(1,128)}), s32[8,1,16]{2,1,0:T(1,128)}, u32[]{:S(2)}, u32[]{:S(2)}) async-start(s32[8,1,16]{2,1,0:T(1,128)} %bitcast.10), calls=%async_computation | async-start | bytes 8192 | tf_op jit(solution)/shard_map/all_to_all | solution.py:171
  33.2 2.1 reshape.396
  39.7 2.1 reshape_reshape.6
  43.3 2.5 copy.51
  47.1 1.4 copy.36
  50.8 2.8 gather_fusion
  53.5 2.2 gather_fusion.2
  55.7 5.1 %all-to-all-start.2 = ((bf16[8,16,64,128]{3,2,1,0:T(8,128)(2,1)}), bf16[8,16,64,128]{3,2,1,0:T(8,128)(2,1)}, u32[]{:S(2)}, u32[]{:S(2)}) async-start(bf16[8,16,64,128]{3,2,1,0:T(8,128)(2,1)} %bitcast.111), calls=%async_computation.2 | async-start | bytes 4194304 | tf_op jit(solution)/shard_map/all_to_all | solution.py:174
  62.6 4.6 %collective-permute-start.1 = (bf16[204800]{0:T(1024)(128)(2,1)}, bf16[204800]{0:T(1024)(128)(2,1)}, u32[]{:S(2)}, u32[]{:S(2)}) collective-permute-start(bf16[204800]{0:T(1024)(128)(2,1)} %pad_maximum_fusion), channel_id=1, source_target_pairs={{0,4},{1,5},{2,6},{3,7},{8,12},{9,13},{10,14},{11,15},{16,20},{17,... | collective-permute-start | bytes 1228808 | tf_op jit(solution)/shard_map/ppermute | solution.py:21
  67.2 3.6 %collective-permute-start.2 = (bf16[204800]{0:T(1024)(128)(2,1)}, bf16[204800]{0:T(1024)(128)(2,1)}, u32[]{:S(2)}, u32[]{:S(2)}) collective-permute-start(bf16[204800]{0:T(1024)(128)(2,1)} %pad_maximum_fusion), channel_id=1, source_target_pairs={{0,3},{1,4},{2,5},{3,6},{4,7},{8,11},{9,12},{10,13},{11,14},{12,15... | collective-permute-start | bytes 1228808 | tf_op jit(solution)/shard_map/ppermute | solution.py:21
  70.8 2.6 collective-permute-start.3
  73.4 2.1 collective-permute-start.4
  81.6 23.1 %collective-permute-done.1 = bf16[204800]{0:T(1024)(128)(2,1)} collective-permute-done((bf16[204800]{0:T(1024)(128)(2,1)}, bf16[204800]{0:T(1024)(128)(2,1)}, u32[]{:S(2)}, u32[]{:S(2)}) %collective-permute-start.1) | collective-permute-done | bytes 409632 | tf_op jit(solution)/shard_map/ppermute | solution.py:21
  104.7 1.4 fusion.57
  106.1 7.4 %collective-permute-done.2 = bf16[204800]{0:T(1024)(128)(2,1)} collective-permute-done((bf16[204800]{0:T(1024)(128)(2,1)}, bf16[204800]{0:T(1024)(128)(2,1)}, u32[]{:S(2)}, u32[]{:S(2)}) %collective-permute-start.2) | collective-permute-done | bytes 409632 | tf_op jit(solution)/shard_map/ppermute | solution.py:21
  114.8 7.4 %collective-permute-done.3 = bf16[204800]{0:T(1024)(128)(2,1)} collective-permute-done((bf16[204800]{0:T(1024)(128)(2,1)}, bf16[204800]{0:T(1024)(128)(2,1)}, u32[]{:S(2)}, u32[]{:S(2)}) %collective-permute-start.3) | collective-permute-done | bytes 409632 | tf_op jit(solution)/shard_map/ppermute | solution.py:21
  122.3 1.4 fusion.49
  123.7 1.4 fusion.55
  126.4 33.3 %all-to-all-start.1 = ((bf16[8,16,64,192]{3,2,1,0:T(8,128)(2,1)}), bf16[8,16,64,192]{3,2,1,0:T(8,128)(2,1)}, u32[]{:S(2)}, u32[]{:S(2)}) async-start(bf16[8,16,64,192]{3,2,1,0:T(8,128)(2,1)} %bitcast.108), calls=%async_computation.1 | async-start | bytes 8388608 | tf_op jit(solution)/shard_map/all_to_all | solution.py:173
  164.9 3.2 %fusion.68 = (f32[2048]{0:T(1024)S(1)}, f32[2048,1152]{0,1:T(8,128)S(1)}) fusion(pred[2048,1152]{0,1:T(32,128)(4,1)S(1)} %copy.51, bf16[1152,192]{1,0:T(8,128)(2,1)S(1)} %constant_dynamic-update-slice_fusion.1, bf16[2048,192]{1,0:T(8,128)(2,1)} %reshape.396), kind=kOutput, calls=%fused_computation.130 | convolution fusion | flops 913045504 | bytes 13033472 | tf_op jit(solution)/shard_map/rd,kd->rk/dot_general | solution.py:199
  169.5 2.8 fusion.16
  176.0 1.8 fusion.23
  177.8 1.9 fusion.30
  179.8 81.4 %all_gather.11 = bf16[512,320]{1,0:T(8,128)(2,1)S(1)} all-gather(bf16[64,320]{1,0:T(8,128)(2,1)S(1)} %pad_maximum_fusion.4), channel_id=1, replica_groups=mesh['kv'=4,'seq'=8] {'seq'}, dimensions={0}, use_global_device_ids=true | all-gather | bytes 368640 | tf_op jit(solution)/shard_map/all_gather | solution.py:130
  263.1 1.5 fusion.15
  265.8 3.4 %gather_fusion.3 = bf16[64,64,128]{2,1,0:T(8,128)(2,1)} fusion(bf16[128,64,128]{2,1,0:T(8,128)(2,1)} %bitcast.20, s32[1024]{0:T(1024)} %pad_clamp_fusion), kind=kCustom, calls=%fused_computation.3 | custom fusion | bytes 2097408 | tf_op jit(solution)/shard_map/gather | solution.py:180
  269.2 3.0 %gather_fusion.1 = bf16[64,64,192]{2,1,0:T(8,128)(2,1)S(1)} fusion(bf16[128,64,192]{2,1,0:T(8,128)(2,1)} %bitcast.14, s32[1024]{0:T(1024)} %pad_clamp_fusion), kind=kCustom, calls=%fused_computation.1 | custom fusion | bytes 3145984 | tf_op jit(solution)/shard_map/gather | solution.py:179
  273.5 1.4 fusion.3
  274.9 3.2 %fusion.41 = f32[4,512,128]{2,1,0:T(8,128)} fusion(bf16[4,1024,128]{2,1,0:T(8,128)(2,1)S(1)} %bitcast.117, f32[4,1024,512]{2,1,0:T(8,128)S(1)} %get-tuple-element.17, f32[4,512]{1,0:T(4,128)S(1)} %get-tuple-element.16, f32[4,512]{1,0:T(4,128)S(1)} %fusion.3), kind=kOutput, calls=%fused_computation.50 | convolution fusion | flops 543424512 | bytes 10502144 | tf_op jit(solution)/shard_map/dot_general | solution.py:38
  278.1 1.5 reshape_reshape.7
  280.7 1.9 fusion.39
  (153 shorter events, 45.6 us)
Async XLA Ops:
  6.5 25.1 %copy-start.6 = (bf16[1024,192]{0,1:T(8,128)(2,1)S(1)}, bf16[1024,192]{0,1:T(8,128)(2,1)}, u32[]{:S(2)}) copy-start(bf16[1024,192]{0,1:T(8,128)(2,1)} %param.10) | copy-start | bytes 1179652
  6.5 25.4 %copy-start = (bf16[1024,128]{1,0:T(8,128)(2,1)S(1)}, bf16[1024,128]{1,0:T(8,128)(2,1)}, u32[]{:S(2)}) copy-start(bf16[1024,128]{1,0:T(8,128)(2,1)} %param.11) | copy-start | bytes 786436
  6.5 26.7 %copy-start.1 = (bf16[128,3072]{1,0:T(8,128)(2,1)S(1)}, bf16[128,3072]{1,0:T(8,128)(2,1)}, u32[]{:S(2)}) copy-start(bf16[128,3072]{1,0:T(8,128)(2,1)} %param.9) | copy-start | bytes 2359300
  6.5 166.9 %all-gather.5.cloned.1.call-start = ((), (), s32[]{:S(2)}) async-start(), calls=%async_computation.4 | async-start | bytes 1310720 | tf_op jit(solution)/shard_map/all_gather | solution.py:66
  8.3 29.3 %copy-start.19 = (bf16[16,192,3]{1,0,2:T(8,128)(2,1)S(1)}, bf16[16,192,3]{1,0,2:T(8,128)(2,1)}, u32[]{:S(2)}) copy-start(bf16[16,192,3]{1,0,2:T(8,128)(2,1)} %param.17) | copy-start | bytes 55300
  10.4 50.4 %collective-permute-start = (bf16[163840]{0:T(1024)(128)(2,1)}, bf16[163840]{0:T(1024)(128)(2,1)}, u32[]{:S(2)}, u32[]{:S(2)}) collective-permute-start(bf16[163840]{0:T(1024)(128)(2,1)} %pad_maximum_fusion.2), channel_id=1, source_target_pairs={{7,0},{0,1},{1,2},{2,3},{3,4},{4,5},{5,6},{6,7},{15,8},{8,9},{9,10... | collective-permute-start | bytes 983048 | tf_op jit(solution)/shard_map/ppermute | solution.py:15
  24.7 25.3 %all-to-all-start = ((s32[8,1,16]{2,1,0:T(1,128)}), s32[8,1,16]{2,1,0:T(1,128)}, u32[]{:S(2)}, u32[]{:S(2)}) async-start(s32[8,1,16]{2,1,0:T(1,128)} %bitcast.10), calls=%async_computation | async-start | bytes 8192 | tf_op jit(solution)/shard_map/all_to_all | solution.py:171
  30.9 145.2 %all-gather.3.cloned.1.call-start = ((), (), s32[]{:S(2)}) async-start(), calls=%async_computation.3 | async-start | bytes 2949120 | tf_op jit(solution)/shard_map/all_gather | solution.py:65
  31.6 10.2 %copy-start.18 = (bf16[128,192]{0,1:T(8,128)(2,1)S(1)}, bf16[128,192]{0,1:T(8,128)(2,1)}, u32[]{:S(2)}) copy-start(bf16[128,192]{0,1:T(8,128)(2,1)} %param.12) | copy-start | bytes 147460
  41.9 1.4 copy-start.9
  53.5 8.3 %copy-start.15 = (bf16[24576]{0:T(1024)(128)(2,1)S(1)}, bf16[24576]{0:T(1024)(128)(2,1)}, u32[]{:S(2)}) copy-start(bf16[24576]{0:T(1024)(128)(2,1)} %reshape.406) | copy-start | bytes 147460
  53.5 8.3 %copy-start.16 = (bf16[128,128]{1,0:T(8,128)(2,1)S(1)}, bf16[128,128]{1,0:T(8,128)(2,1)}, u32[]{:S(2)}) copy-start(bf16[128,128]{1,0:T(8,128)(2,1)} %param.13) | copy-start | bytes 98308
  55.7 70.7 %all-to-all-start.2 = ((bf16[8,16,64,128]{3,2,1,0:T(8,128)(2,1)}), bf16[8,16,64,128]{3,2,1,0:T(8,128)(2,1)}, u32[]{:S(2)}, u32[]{:S(2)}) async-start(bf16[8,16,64,128]{3,2,1,0:T(8,128)(2,1)} %bitcast.111), calls=%async_computation.2 | async-start | bytes 4194304 | tf_op jit(solution)/shard_map/all_to_all | solution.py:174
  62.6 42.1 %collective-permute-start.1 = (bf16[204800]{0:T(1024)(128)(2,1)}, bf16[204800]{0:T(1024)(128)(2,1)}, u32[]{:S(2)}, u32[]{:S(2)}) collective-permute-start(bf16[204800]{0:T(1024)(128)(2,1)} %pad_maximum_fusion), channel_id=1, source_target_pairs={{0,4},{1,5},{2,6},{3,7},{8,12},{9,13},{10,14},{11,15},{16,20},{17,... | collective-permute-start | bytes 1228808 | tf_op jit(solution)/shard_map/ppermute | solution.py:21
  67.2 46.3 %collective-permute-start.2 = (bf16[204800]{0:T(1024)(128)(2,1)}, bf16[204800]{0:T(1024)(128)(2,1)}, u32[]{:S(2)}, u32[]{:S(2)}) collective-permute-start(bf16[204800]{0:T(1024)(128)(2,1)} %pad_maximum_fusion), channel_id=1, source_target_pairs={{0,3},{1,4},{2,5},{3,6},{4,7},{8,11},{9,12},{10,13},{11,14},{12,15... | collective-permute-start | bytes 1228808 | tf_op jit(solution)/shard_map/ppermute | solution.py:21
  70.8 51.5 %collective-permute-start.3 = (bf16[204800]{0:T(1024)(128)(2,1)}, bf16[204800]{0:T(1024)(128)(2,1)}, u32[]{:S(2)}, u32[]{:S(2)}) collective-permute-start(bf16[204800]{0:T(1024)(128)(2,1)} %pad_maximum_fusion), channel_id=1, source_target_pairs={{0,2},{1,3},{2,4},{3,5},{4,6},{5,7},{8,10},{9,11},{10,12},{11,13},... | collective-permute-start | bytes 1228808 | tf_op jit(solution)/shard_map/ppermute | solution.py:21
  73.4 48.9 %collective-permute-start.4 = (bf16[204800]{0:T(1024)(128)(2,1)}, bf16[204800]{0:T(1024)(128)(2,1)}, u32[]{:S(2)}, u32[]{:S(2)}) collective-permute-start(bf16[204800]{0:T(1024)(128)(2,1)} %pad_maximum_fusion), channel_id=1, source_target_pairs={{0,1},{1,2},{2,3},{3,4},{4,5},{5,6},{6,7},{8,9},{9,10},{10,11},{11... | collective-permute-start | bytes 1228808 | tf_op jit(solution)/shard_map/ppermute | solution.py:21
  126.4 37.8 %copy-start.17 = (bf16[128,128]{1,0:T(8,128)(2,1)S(1)}, bf16[128,128]{1,0:T(8,128)(2,1)}, u32[]{:S(2)}) copy-start(bf16[128,128]{1,0:T(8,128)(2,1)} %param.13) | copy-start | bytes 98308
  126.4 38.4 %copy-start.10 = (bf16[128,192]{1,0:T(8,128)(2,1)S(1)}, bf16[128,192]{1,0:T(8,128)(2,1)}, u32[]{:S(2)}) copy-start(bf16[128,192]{1,0:T(8,128)(2,1)} %copy-done.9) | copy-start | bytes 147460
  126.4 142.7 %all-to-all-start.1 = ((bf16[8,16,64,192]{3,2,1,0:T(8,128)(2,1)}), bf16[8,16,64,192]{3,2,1,0:T(8,128)(2,1)}, u32[]{:S(2)}, u32[]{:S(2)}) async-start(bf16[8,16,64,192]{3,2,1,0:T(8,128)(2,1)} %bitcast.108), calls=%async_computation.1 | async-start | bytes 8388608 | tf_op jit(solution)/shard_map/all_to_all | solution.py:173
  169.5 5.3 %copy-start.8 = (bf16[64,2048]{1,0:T(8,128)(2,1)S(1)}, bf16[64,2048]{1,0:T(8,128)(2,1)}, u32[]{:S(2)}) copy-start(bf16[64,2048]{1,0:T(8,128)(2,1)} %reshape.395) | copy-start | bytes 786436
  169.5 6.6 %copy-start.11 = (bf16[64,3072]{1,0:T(8,128)(2,1)S(1)}, bf16[64,3072]{1,0:T(8,128)(2,1)}, u32[]{:S(2)}) copy-start(bf16[64,3072]{1,0:T(8,128)(2,1)} %reshape.393) | copy-start | bytes 1179652
  172.3 88.9 %copy-start.2 = (bf16[2048,192]{1,0:T(8,128)(2,1)S(1)}, bf16[2048,192]{1,0:T(8,128)(2,1)}, u32[]{:S(2)}) copy-start(bf16[2048,192]{1,0:T(8,128)(2,1)} %reshape.396) | copy-start | bytes 2359300
  172.3 88.9 %copy-start.20 = (pred[512]{0:T(512)(128)(4,1)S(1)}, pred[512]{0:T(512)(128)(4,1)}, u32[]{:S(2)}) copy-start(pred[512]{0:T(512)(128)(4,1)} %iota_compare_fusion.1) | copy-start | bytes 1540
  264.6 7.6 %copy-start.3 = (bf16[4,512,192]{2,1,0:T(8,128)(2,1)S(1)}, bf16[4,512,192]{2,1,0:T(8,128)(2,1)}, u32[]{:S(2)}) copy-start(bf16[4,512,192]{2,1,0:T(8,128)(2,1)} %reshape_reshape.6) | copy-start | bytes 2359300
  273.5 1.4 copy-start.7
  274.9 4.8 %copy-start.12 = (f32[128,16]{1,0:T(8,128)S(1)}, f32[128,16]{1,0:T(8,128)}, u32[]{:S(2)}) copy-start(f32[128,16]{1,0:T(8,128)} %copy.36) | copy-start | bytes 24580
  274.9 5.1 %copy-start.13 = (f32[128,16]{1,0:T(8,128)S(1)}, f32[128,16]{1,0:T(8,128)}, u32[]{:S(2)}) copy-start(f32[128,16]{1,0:T(8,128)} %copy.41) | copy-start | bytes 24580
  278.1 2.2 copy-start.14
  278.1 2.6 copy-start.4
  278.1 2.6 copy-start.5
Sparse Core Ops, SparseCore 0:
  9.2 29.2 all-gather.4
  40.3 37.3 all-gather.2
